TPU v7x, 128 devices: a whole 4x4x4 slice. The times are simulated.
128 devices in a mesh: section: 4 (over x), dev: 32 (over y, z, core).
Axes of the slice: x: 4, y: 4, z: 4, core: 2. Of those that a mesh axis runs over, the one named last changes fastest.
Arguments:
- hidden: bfloat16 [1024, 2048], P('dev'), may hold values from -8 to 8
- lengths: int32 [1024], P('dev'), may hold values from 1 to 256, as said below
- attn_gain: float32 [2048], replicated, may hold values from 0.1 to 1.9
- w_query: bfloat16 [2048, 3072], P(None, 'section'), may hold values from -0.125 to 0.125
- w_latent: bfloat16 [2048, 512], replicated, may hold values from -0.125 to 0.125
- latent_gain: float32 [512], replicated, may hold values from 0.1 to 1.9
- w_rope_key: bfloat16 [64, 2048], replicated, may hold values from -0.125 to 0.125
- w_key_up: bfloat16 [16, 512, 128], P('section'), may hold values from -0.5 to 0.5
- w_value_up: bfloat16 [16, 512, 128], P('section'), may hold values from -0.25 to 0.25
- w_out: bfloat16 [2048, 2048], P('section'), may hold values from -0.125 to 0.125
- latent_cache: bfloat16 [1024, 256, 512], P('dev'), may hold values from -6 to 6
- rope_cache: bfloat16 [1024, 64, 256], P('dev'), may hold values from -1200 to 1200
- ffn_gain: float32 [2048], replicated, may hold values from 0.1 to 1.9
- expert_ids: int32 [1024, 6], P('dev'), may hold values from 0 to 63, all different within a row; in each aligned block of 8 rows (0 to 7, 8 to 15, ...) at most 2 rows name the same one
- route_weights: float32 [1024, 6], P('dev'), may hold values from 0.05 to 0.5
- w_gate_up: bfloat16 [64, 2, 1408, 2048], P('dev', None, 'section'), may hold values from -0.125 to 0.125
- w_down: bfloat16 [64, 1408, 2048], P('dev', 'section'), may hold values from -0.15625 to 0.15625
Outputs:
- layer_out: bfloat16 [1024, 2048], P('dev')
Inputs may be any that keep to these rules, and one draw needn't show every extreme that they name: `lengths`: every aligned block of 32 rows holds a row of length 256. `expert_ids`: each row names 6 different experts. In every aligned block of 8 rows no expert is named by more than 2 rows, and some block has an expert named by exactly 2.
All inputs are finite; a program needn't handle non-finite values.
Results may differ from a plain program's by a relative error of at most 0.011.
Values may be sent and summed in bfloat16 or wider, within the bound.
No kernel may reach another device: no remote copies, remote signals or barrier semaphores. Data moves between devices by JAX's collectives and lax.ppermute only.
A program may use at most 128 MiB of HBM per device.

v0:
```python
import jax
import jax.numpy as jnp
from jax import lax
from jax.sharding import PartitionSpec as P

EXPERTS = 64
MOST = 2
epsilon = 1e-06
far_below = -1e30


def rms_norm(values, norm_gain):
    mean_square = jnp.mean(values * values, axis=-1, keepdims=True)
    return values * lax.rsqrt(mean_square + epsilon) * norm_gain


def rotary(values, positions):
    half_width = values.shape[-1] // 2
    step_index = jnp.arange(half_width, dtype=jnp.float32)
    frequency = jnp.exp(-jnp.log(10000.0) * step_index / half_width)
    angles = positions.astype(jnp.float32)[:, None] * frequency[None, :]
    if values.ndim == 3:
        angles = angles[:, None, :]
    cosine = jnp.cos(angles)
    sine_part = jnp.sin(angles)
    first_half = values[..., :half_width]
    second = values[..., half_width:]
    return jnp.concatenate(
        [first_half * cosine - second * sine_part, second * cosine + first_half * sine_part],
        axis=-1,
    )


def slot_targets(expert_ids, block_rows):
    row_count, top_count = expert_ids.shape
    blocks = row_count // block_rows
    flat_ids = expert_ids.reshape(blocks, block_rows * top_count)
    onehot = (flat_ids[:, :, None] == jnp.arange(EXPERTS, dtype=jnp.int32)[None, None, :]).astype(
        jnp.int32
    )
    earlier = jnp.cumsum(onehot, axis=1) - onehot
    rank_in = jnp.sum(earlier * onehot, axis=2)
    capacity = blocks * MOST
    target = flat_ids * capacity + jnp.arange(blocks, dtype=jnp.int32)[:, None] * MOST + rank_in
    return (target.reshape(row_count, top_count), capacity)


def pack_rows(source, target, capacity):
    slot_count = EXPERTS * capacity
    hit_table = (
        target[:, :, None] == jnp.arange(slot_count, dtype=jnp.int32)[None, None, :]
    ).astype(jnp.bfloat16)
    hit_table = jnp.sum(hit_table, axis=1)
    packed = lax.dot_general(
        hit_table, source, (((0,), (0,)), ((), ())), preferred_element_type=jnp.float32
    )
    return packed.astype(jnp.bfloat16)


def expert_part(slot_rows, w_gate_up, w_down):
    gate_up = jnp.einsum(
        "secx,egfx->secgf", slot_rows, w_gate_up, preferred_element_type=jnp.float32
    )
    activated = (jax.nn.silu(gate_up[:, :, :, 0, :]) * gate_up[:, :, :, 1, :]).astype(jnp.bfloat16)
    return jnp.einsum("secf,efx->secx", activated, w_down, preferred_element_type=jnp.float32)


def combine_rows(middle, expert_out, target, route_weights):
    flat_out = expert_out.reshape(-1, expert_out.shape[-1])
    routed = jnp.take(flat_out, target.reshape(-1), axis=0)
    routed = routed.reshape(target.shape + (flat_out.shape[1],)).astype(jnp.float32)
    layer_out = middle.astype(jnp.float32) + jnp.sum(route_weights[:, :, None] * routed, axis=1)
    return layer_out.astype(jnp.bfloat16)


def attend(
    query_latent, query_rope, latent_new, key_new, latent_cache, rope_cache, lengths, score_scale
):
    scores = jnp.einsum(
        "rhl,rtl->rht", query_latent, latent_cache, preferred_element_type=jnp.float32
    )
    scores = scores + jnp.einsum(
        "rhp,rpt->rht", query_rope, rope_cache, preferred_element_type=jnp.float32
    )
    scores = scores * score_scale
    self_score = jnp.einsum(
        "rhl,rl->rh", query_latent, latent_new, preferred_element_type=jnp.float32
    )
    self_score = (
        self_score
        + jnp.einsum("rhp,rp->rh", query_rope, key_new, preferred_element_type=jnp.float32)
    ) * score_scale
    places = jnp.arange(latent_cache.shape[1], dtype=jnp.int32)
    valid_mask = places[None, None, :] < lengths[:, None, None]
    masked = jnp.where(valid_mask, scores, far_below)
    peak_score = jnp.maximum(jnp.max(masked, axis=2), self_score)
    weights = jnp.where(valid_mask, jnp.exp(masked - peak_score[:, :, None]), 0.0)
    self_weight = jnp.exp(self_score - peak_score)
    totals = jnp.sum(weights, axis=2) + self_weight
    prob_cache = (weights / totals[:, :, None]).astype(jnp.bfloat16)
    prob_self = (self_weight / totals).astype(jnp.bfloat16)
    mixed = jnp.einsum("rht,rtl->rhl", prob_cache, latent_cache, preferred_element_type=jnp.float32)
    mixed = (
        mixed
        + prob_self.astype(jnp.float32)[:, :, None] * latent_new.astype(jnp.float32)[:, None, :]
    )
    return mixed.astype(jnp.bfloat16)


def per_device(
    hidden,
    lengths,
    attn_gain,
    w_query,
    w_latent,
    latent_gain,
    w_rope_key,
    w_key_up,
    w_value_up,
    w_out,
    latent_cache,
    rope_cache,
    ffn_gain,
    expert_ids,
    route_weights,
    w_gate_up,
    w_down,
):
    sections = lax.axis_size("section")
    devices = lax.axis_size("dev")
    row_count = hidden.shape[0]
    quarter = row_count // sections
    model_width = hidden.shape[1]
    head_local = w_key_up.shape[0]
    nope_width = w_key_up.shape[2]
    rope_width = w_rope_key.shape[0]
    score_scale = (nope_width + rope_width) ** (-0.5)
    normed = rms_norm(hidden.astype(jnp.float32), attn_gain).astype(jnp.bfloat16)
    queries = jnp.dot(normed, w_query, preferred_element_type=jnp.float32).astype(jnp.bfloat16)
    queries = queries.reshape(row_count, head_local, nope_width + rope_width)
    query_rope = rotary(queries[:, :, nope_width:].astype(jnp.float32), lengths).astype(
        jnp.bfloat16
    )
    query_latent = jnp.einsum(
        "rhn,hln->rhl", queries[:, :, :nope_width], w_key_up, preferred_element_type=jnp.float32
    ).astype(jnp.bfloat16)
    latent_new = rms_norm(
        jnp.dot(normed, w_latent, preferred_element_type=jnp.float32), latent_gain
    ).astype(jnp.bfloat16)
    key_raw = lax.dot_general(
        normed, w_rope_key, (((1,), (1,)), ((), ())), preferred_element_type=jnp.float32
    )
    key_new = rotary(key_raw, lengths).astype(jnp.bfloat16)
    mixed_latent = attend(
        query_latent,
        query_rope,
        latent_new,
        key_new,
        latent_cache,
        rope_cache,
        lengths,
        score_scale,
    )
    head_out = jnp.einsum(
        "rhl,hlv->rhv", mixed_latent, w_value_up, preferred_element_type=jnp.float32
    ).astype(jnp.bfloat16)
    heads_flat = head_out.reshape(row_count, -1)
    partial_value = jnp.dot(heads_flat, w_out, preferred_element_type=jnp.float32)
    attention = lax.psum(partial_value, "section")
    middle = (hidden.astype(jnp.float32) + attention).astype(jnp.bfloat16)
    expert_in = rms_norm(middle.astype(jnp.float32), ffn_gain).astype(jnp.bfloat16)
    target, capacity = slot_targets(expert_ids, quarter)
    packed = pack_rows(expert_in, target, capacity).reshape(devices, -1, capacity, model_width)
    partial_out = expert_part(
        lax.all_to_all(packed, "dev", split_axis=0, concat_axis=0, tiled=True), w_gate_up, w_down
    )
    returned = lax.all_to_all(
        partial_out.astype(jnp.bfloat16), "dev", split_axis=0, concat_axis=0, tiled=True
    ).astype(partial_out.dtype)
    expert_out = lax.psum(returned.astype(jnp.bfloat16), "section")
    return combine_rows(middle, expert_out, target, route_weights)


def solution(mesh):
    in_specs = (
        P("dev", None),
        P("dev"),
        P(),
        P(None, "section"),
        P(),
        P(),
        P(),
        P("section", None, None),
        P("section", None, None),
        P("section", None),
        P("dev", None, None),
        P("dev", None, None),
        P(),
        P("dev", None),
        P("dev", None),
        P("dev", None, "section", None),
        P("dev", "section", None),
    )
    out_specs = P("dev", None)
    return jax.shard_map(
        per_device, mesh=mesh, in_specs=in_specs, out_specs=out_specs, check_vma=False
    )
```

profile of v0, /device:TPU:1, one launch (start us, length us, event | category | flops | bytes accessed | tf_op | source)
XLA Modules:
  0.0 220.6 jit_solution(4492424188257684018)
XLA Ops:
  6.6 0.5 multiply_exponential_fusion
  7.1 1.3 fusion.22
  8.5 2.2 %convolution_convert_fusion.3 = bf16[32,768]{1,0:T(8,128)(2,1)} fusion(bf16[2048,768]{1,0:T(8,128)(2,1)S(1)} %copy-done, bf16[32,2048]{1,0:T(8,128)(2,1)} %param.17, f32[2048]{0:T(1024)} %param.19, f32[32]{0:T(128)S(1)} %add_rsqrt_fusion.2), kind=kOutput, calls=%fused_computation.17 | convolution fusion | flops 100950016 | bytes 3334272 | tf_op jit(solution)/shard_map/dot_general | solution.py:139
  10.7 1.5 reshape.195
  12.3 0.9 slice_convert_fusion
  13.6 0.9 subtract_convert_fusion.1
  14.9 1.5 fusion.56
  16.5 0.6 multiply_reduce_fusion.1
  17.8 5.9 %fusion.65 = (f32[32,4]{1,0:T(8,128)S(1)}, f32[32,4,256]{2,1,0:T(4,128)S(1)}) fusion(f32[32,4,256]{2,1,0:T(4,128)S(1)} %fusion.56, bf16[32,256,512]{2,1,0:T(8,128)(2,1)} %param.27, bf16[32,4,512]{2,0,1:T(8,128)(2,1)S(1)} %fusion.13, pred[32,256]{1,0:T(8,128)(4,1)S(1)} %iota_compare_fusion.2), kind=kOutput, calls=%fused_computation.101 | convolution fusion | flops 33685376 | bytes 8790528 | tf_op jit(solution)/shard_map/rhl,rtl->rht/dot_general | solution.py:79
  24.0 1.2 fusion.12
  25.7 1.2 fusion.45
  28.1 41.6 %all-reduce.3.cloned.1.call-done = f32[32,2048]{1,0:T(8,128)} async-done(((f32[32,2048]{1,0:T(8,128)}), f32[32,2048]{1,0:T(8,128)}) %all-reduce.3.cloned.1.call-update) | async-done | bytes 262160 | tf_op jit(solution)/shard_map/psum | solution.py:169
  69.7 1.1 fusion.26
  70.9 0.8 convolution_convert_fusion
  71.6 37.8 %all_to_all.10 = bf16[32,2,8,2048]{3,2,1,0:T(8,128)(2,1)S(1)} all-to-all(bf16[32,2,8,2048]{3,2,1,0:T(8,128)(2,1)S(1)} %bitcast.68), channel_id=1, replica_groups=mesh['section'=4,'dev'=32] {'dev'}, dimensions={0} | all-to-all | bytes 4194304 | tf_op jit(solution)/shard_map/all_to_all | solution.py:175
  109.4 4.8 %fusion.7 = f32[32,2,8,2,352]{4,2,3,0,1:T(8,128)S(1)} fusion(bf16[2,2,352,2048]{3,2,1,0:T(8,128)(2,1)} %param.32, bf16[32,2,8,2048]{3,2,1,0:T(8,128)(2,1)S(1)} %all_to_all.10), kind=kOutput, calls=%fused_computation.9 | convolution fusion | flops 1476395008 | bytes 9306112 | tf_op jit(solution)/shard_map/secx,egfx->secgf/dot_general | solution.py:61
  114.2 1.3 fusion.3
  115.8 32.0 %all_to_all.11 = bf16[32,2,8,2048]{3,2,1,0:T(8,128)(2,1)} all-to-all(bf16[32,2,8,2048]{3,2,1,0:T(8,128)(2,1)S(1)} %copy.56), channel_id=1, replica_groups=mesh['section'=4,'dev'=32] {'dev'}, dimensions={0} | all-to-all | bytes 4194304 | tf_op jit(solution)/shard_map/all_to_all | solution.py:177
  148.1 0.3 copy-done.10
  148.6 54.8 %all-reduce.5.cloned.1.call-done = bf16[512,2048]{1,0:T(8,128)(2,1)} async-done(((bf16[512,2048]{1,0:T(8,128)(2,1)}), bf16[512,2048]{1,0:T(8,128)(2,1)}) %all-reduce.5.cloned.1.call-update) | async-done | bytes 2097168 | tf_op jit(solution)/shard_map/psum | solution.py:180
  203.3 4.7 %gather_fusion = bf16[192,2048]{1,0:T(8,128)(2,1)} fusion(bf16[512,2048]{1,0:T(8,128)(2,1)} %all-reduce.5.cloned.1.call-done, s32[1024]{0:T(1024)S(1)} %pad_clamp_fusion), kind=kCustom, calls=%fused_computation | custom fusion | bytes 1573632 | tf_op jit(solution)/shard_map/jit(_take)/gather | solution.py:70
  208.0 2.2 gather.7
  210.2 2.9 %multiply_reduce_fusion = f32[32,2048]{1,0:T(8,128)S(1)} fusion(bf16[32,6,2048]{2,1,0:T(8,128)(2,1)} %gather.7, f32[32,6]{1,0:T(8,128)S(1)} %copy.50, pred[32,6]{1,0:T(8,128)(4,1)S(1)} %get-tuple-element.5), kind=kLoop, calls=%fused_computation.8 | loop fusion | flops 1507328 | bytes 1049536 | tf_op jit(solution)/shard_map/reduce_sum | solution.py:72
  213.1 0.7 fusion.29
  (75 shorter events, 4.1 us)
Async XLA Ops:
  6.5 2.0 copy-start
  6.5 6.8 %copy-start.1 = (bf16[32,2048]{1,0:T(8,128)(2,1)S(1)}, bf16[32,2048]{1,0:T(8,128)(2,1)}, u32[]{:S(2)}) copy-start(bf16[32,2048]{1,0:T(8,128)(2,1)} %param.17) | copy-start | bytes 393220
  6.5 6.8 %copy-start.7 = (f32[2048]{0:T(1024)S(1)}, f32[2048]{0:T(1024)}, u32[]{:S(2)}) copy-start(f32[2048]{0:T(1024)} %param.19) | copy-start | bytes 24580
  6.5 6.6 %copy-start.12 = (s32[32]{0:T(128)S(1)}, s32[32]{0:T(128)}, u32[]{:S(2)}) copy-start(s32[32]{0:T(128)} %param.18) | copy-start | bytes 388
  6.5 6.8 %copy-start.6 = (bf16[64,2048]{1,0:T(8,128)(2,1)S(1)}, bf16[64,2048]{1,0:T(8,128)(2,1)}, u32[]{:S(2)}) copy-start(bf16[64,2048]{1,0:T(8,128)(2,1)} %param.23) | copy-start | bytes 786436
  6.5 63.2 %all-reduce.3.cloned.1.call-start = ((), (), s32[]{:S(2)}) async-start(), calls=%async_computation.2 | async-start | bytes 524288 | tf_op jit(solution)/shard_map/psum | solution.py:169
  12.3 4.2 %copy-start.3 = (bf16[2048,512]{1,0:T(8,128)(2,1)S(1)}, bf16[2048,512]{1,0:T(8,128)(2,1)}, u32[]{:S(2)}) copy-start(bf16[2048,512]{1,0:T(8,128)(2,1)} %param.21) | copy-start | bytes 6291460
  12.3 5.2 %copy-start.11 = (f32[512]{0:T(512)S(1)}, f32[512]{0:T(512)}, u32[]{:S(2)}) copy-start(f32[512]{0:T(512)} %param.22) | copy-start | bytes 6148
  13.2 3.9 %copy-start.4 = (bf16[4,512,128]{2,1,0:T(8,128)(2,1)S(1)}, bf16[4,512,128]{2,1,0:T(8,128)(2,1)}, u32[]{:S(2)}) copy-start(bf16[4,512,128]{2,1,0:T(8,128)(2,1)} %param.24) | copy-start | bytes 1572868
  13.2 3.9 %slice-start.2 = ((bf16[32,4,192]{2,1,0:T(4,128)(2,1)}), bf16[32,4,128]{2,1,0:T(4,128)(2,1)S(1)}, s32[]{:S(2)}) async-start(bf16[32,4,192]{2,1,0:T(4,128)(2,1)} %reshape.195), calls=%async_computation.6 | async-start | bytes 65536 | tf_op jit(solution)/shard_map/slice | solution.py:145
  13.3 10.6 %slice-start = ((s8[8388608]{0:T(1024)(128)(4,1)}), s8[4194304]{0:T(1024)(128)(4,1)S(1)}, s32[]{:S(2)}) async-start(s8[8388608]{0:T(1024)(128)(4,1)} %bitcast.65), calls=%async_computation.4 | async-start | bytes 8388608
  17.8 6.2 %slice-start.1 = ((s8[8388608]{0:T(1024)(128)(4,1)}), s8[4194304]{0:T(1024)(128)(4,1)S(1)}, s32[]{:S(2)}) async-start(s8[8388608]{0:T(1024)(128)(4,1)} %bitcast.65), calls=%async_computation.5 | async-start | bytes 8388608
  23.9 1.3 copy-start.5
  24.0 1.8 copy-start.2
  25.2 1.8 copy-start.9
  25.2 45.6 %copy-start.8 = (f32[2048]{0:T(1024)S(1)}, f32[2048]{0:T(1024)}, u32[]{:S(2)}) copy-start(f32[2048]{0:T(1024)} %param.29) | copy-start | bytes 24580
  26.9 176.4 %all-reduce.5.cloned.1.call-start = ((), (), s32[]{:S(2)}) async-start(), calls=%async_computation.3 | async-start | bytes 4194304 | tf_op jit(solution)/shard_map/psum | solution.py:180
  109.4 4.8 %copy-start.13 = (bf16[2,352,2048]{2,1,0:T(8,128)(2,1)S(1)}, bf16[2,352,2048]{2,1,0:T(8,128)(2,1)}, u32[]{:S(2)}) copy-start(bf16[2,352,2048]{2,1,0:T(8,128)(2,1)} %param.33) | copy-start | bytes 8650756
  147.8 0.7 copy-start.10
Sparse Core Ops, SparseCore 0:
  27.0 42.6 all-reduce.2
  147.9 55.3 all-reduce.4
where the time goes:
time: 221 us
  waiting for transfers between devices  96.4 us (44%)
  blocking collectives  69.8 us (32%)
  matrix products  20.7 us (9%)
  between operations  13.7 us (6%)
  local copies, waits for them, and re-layouts  10.3 us (5%)
  other arithmetic  9.69 us (4%)
    psum x1, waiting for transfers between devices, per_device(): expert_out = lax.psum(returned.astype(jnp.bfloat16), 'section')  54.8 us
    psum x1, waiting for transfers between devices, per_device(): attention = lax.psum(partial_value, 'section')  41.6 us
    all_to_all x1, blocking collectives, per_device(): lax.all_to_all(packed, 'dev', split_axis=0, concat_axis=0, tiled=True)  37.8 us
    all_to_all x1, blocking collectives, per_device(): lax.all_to_all(partial_out.astype(jnp.bfloat16), 'dev', split_axis=0, con...  32 us
    gather x2, local copies, waits for them, and re-layouts, combine_rows(): routed = jnp.take(flat_out, target.reshape(-1), axis=0)  6.85 us
    dot_general x1, matrix products, attend(): jnp.einsum('rhl,rtl->rht', query_latent, latent_cache, preferred_element_...  5.89 us
    dot_general x1, matrix products, expert_part(): jnp.einsum('secx,egfx->secgf', slot_rows, w_gate_up, preferred_element_ty...  4.8 us
  transfers between devices with their start and end apart: 2, of which 2 were waited for; matrix products, arithmetic and copies ran while one was open for 1% of the time, Pallas kernels for 0%

commit v1 on v0

--- a/solution.py
+++ b/solution.py
@@ -166,7 +166,8 @@
     ).astype(jnp.bfloat16)
     heads_flat = head_out.reshape(row_count, -1)
     partial_value = jnp.dot(heads_flat, w_out, preferred_element_type=jnp.float32)
-    attention = lax.psum(partial_value, "section")
+    pieces = lax.all_gather(partial_value, "section")
+    attention = jnp.sum(pieces, axis=0)
     middle = (hidden.astype(jnp.float32) + attention).astype(jnp.bfloat16)
     expert_in = rms_norm(middle.astype(jnp.float32), ffn_gain).astype(jnp.bfloat16)
     target, capacity = slot_targets(expert_ids, quarter)

time: 221 us -> 205 us (0.928)
  waiting for transfers between devices: 96.4 us -> 79.9 us
    psum x1 -> x0, waiting for transfers between devices: 41.6 us -> none  [per_device(): attention = lax.psum(partial_value, 'section')]
    all_gather x0 -> x1, waiting for transfers between devices: none -> 25.2 us  [per_device(): pieces = lax.all_gather(partial_value, 'section')]
where the time goes in v1:
time: 205 us
  waiting for transfers between devices  79.9 us (39%)
  blocking collectives  68.6 us (33%)
  matrix products  20.7 us (10%)
  between operations  13.7 us (7%)
  other arithmetic  11.7 us (6%)
  local copies, waits for them, and re-layouts  10.3 us (5%)
    psum x1, waiting for transfers between devices, per_device(): expert_out = lax.psum(returned.astype(jnp.bfloat16), 'section')  54.6 us
    all_to_all x1, blocking collectives, per_device(): lax.all_to_all(packed, 'dev', split_axis=0, concat_axis=0, tiled=True)  36.6 us
    all_to_all x1, blocking collectives, per_device(): lax.all_to_all(partial_out.astype(jnp.bfloat16), 'dev', split_axis=0, con...  32 us
    all_gather x1, waiting for transfers between devices, per_device(): pieces = lax.all_gather(partial_value, 'section')  25.2 us
    gather x2, local copies, waits for them, and re-layouts, combine_rows(): routed = jnp.take(flat_out, target.reshape(-1), axis=0)  6.85 us
    dot_general x1, matrix products, attend(): jnp.einsum('rhl,rtl->rht', query_latent, latent_cache, preferred_element_...  5.89 us
    dot_general x1, matrix products, expert_part(): jnp.einsum('secx,egfx->secgf', slot_rows, w_gate_up, preferred_element_ty...  4.8 us
  transfers between devices with their start and end apart: 2, of which 2 were waited for; matrix products, arithmetic and copies ran while one was open for 1% of the time, Pallas kernels for 0%

profile of v1, /device:TPU:1, one launch (start us, length us, event | category | flops | bytes accessed | tf_op | source)
XLA Modules:
  0.0 204.9 jit_solution(13336655803756708709)
XLA Ops:
  6.6 0.5 multiply_exponential_fusion
  7.1 1.3 fusion.22
  8.5 2.2 %convolution_convert_fusion.3 = bf16[32,768]{1,0:T(8,128)(2,1)} fusion(bf16[2048,768]{1,0:T(8,128)(2,1)S(1)} %copy-done, bf16[32,2048]{1,0:T(8,128)(2,1)} %param.17, f32[2048]{0:T(1024)} %param.19, f32[32]{0:T(128)S(1)} %add_rsqrt_fusion.2), kind=kOutput, calls=%fused_computation.17 | convolution fusion | flops 100950016 | bytes 3334272 | tf_op jit(solution)/shard_map/dot_general | solution.py:139
  10.7 1.5 reshape.195
  12.3 0.9 slice_convert_fusion
  13.6 0.9 subtract_convert_fusion.1
  14.9 1.5 fusion.56
  16.5 0.6 multiply_reduce_fusion.1
  17.8 5.9 %fusion.65 = (f32[32,4]{1,0:T(8,128)S(1)}, f32[32,4,256]{2,1,0:T(4,128)S(1)}) fusion(f32[32,4,256]{2,1,0:T(4,128)S(1)} %fusion.56, bf16[32,256,512]{2,1,0:T(8,128)(2,1)} %param.27, bf16[32,4,512]{2,0,1:T(8,128)(2,1)S(1)} %fusion.13, pred[32,256]{1,0:T(8,128)(4,1)S(1)} %iota_compare_fusion.2), kind=kOutput, calls=%fused_computation.101 | convolution fusion | flops 33685376 | bytes 8790528 | tf_op jit(solution)/shard_map/rhl,rtl->rht/dot_general | solution.py:79
  24.0 1.2 fusion.12
  25.7 1.2 fusion.45
  28.1 25.2 %all-gather.3.cloned.1.call-done = f32[128,2048]{1,0:T(8,128)} async-done(((f32[32,2048]{1,0:T(8,128)}), f32[128,2048]{1,0:T(8,128)}) %all-gather.3.cloned.1.call-update) | async-done | bytes 1048592 | tf_op jit(solution)/shard_map/all_gather | solution.py:169
  53.4 2.0 reduce_sum.82
  55.4 1.1 fusion.26
  56.5 0.8 convolution_convert_fusion
  57.3 36.6 %all_to_all.10 = bf16[32,2,8,2048]{3,2,1,0:T(8,128)(2,1)S(1)} all-to-all(bf16[32,2,8,2048]{3,2,1,0:T(8,128)(2,1)S(1)} %bitcast.69), channel_id=1, replica_groups=mesh['section'=4,'dev'=32] {'dev'}, dimensions={0} | all-to-all | bytes 4194304 | tf_op jit(solution)/shard_map/all_to_all | solution.py:176
  93.8 4.8 %fusion.7 = f32[32,2,8,2,352]{4,2,3,0,1:T(8,128)S(1)} fusion(bf16[2,2,352,2048]{3,2,1,0:T(8,128)(2,1)} %param.32, bf16[32,2,8,2048]{3,2,1,0:T(8,128)(2,1)S(1)} %all_to_all.10), kind=kOutput, calls=%fused_computation.9 | convolution fusion | flops 1476395008 | bytes 9306112 | tf_op jit(solution)/shard_map/secx,egfx->secgf/dot_general | solution.py:61
  98.7 1.3 fusion.3
  100.2 32.0 %all_to_all.11 = bf16[32,2,8,2048]{3,2,1,0:T(8,128)(2,1)} all-to-all(bf16[32,2,8,2048]{3,2,1,0:T(8,128)(2,1)S(1)} %copy.56), channel_id=1, replica_groups=mesh['section'=4,'dev'=32] {'dev'}, dimensions={0} | all-to-all | bytes 4194304 | tf_op jit(solution)/shard_map/all_to_all | solution.py:178
  133.0 54.6 %all-reduce.2.cloned.1.call-done = bf16[512,2048]{1,0:T(8,128)(2,1)} async-done(((bf16[512,2048]{1,0:T(8,128)(2,1)}), bf16[512,2048]{1,0:T(8,128)(2,1)}) %all-reduce.2.cloned.1.call-update) | async-done | bytes 2097168 | tf_op jit(solution)/shard_map/psum | solution.py:181
  187.6 4.7 %gather_fusion = bf16[192,2048]{1,0:T(8,128)(2,1)} fusion(bf16[512,2048]{1,0:T(8,128)(2,1)} %all-reduce.2.cloned.1.call-done, s32[1024]{0:T(1024)S(1)} %pad_clamp_fusion), kind=kCustom, calls=%fused_computation | custom fusion | bytes 1573632 | tf_op jit(solution)/shard_map/jit(_take)/gather | solution.py:70
  192.3 2.2 %gather.7 = bf16[32,6,2048]{2,1,0:T(8,128)(2,1)} reshape(bf16[192,2048]{1,0:T(8,128)(2,1)} %gather_fusion) | data formatting | bytes 1572864 | tf_op jit(solution)/shard_map/jit(_take)/gather | solution.py:70
  194.5 2.9 %multiply_reduce_fusion = f32[32,2048]{1,0:T(8,128)S(1)} fusion(bf16[32,6,2048]{2,1,0:T(8,128)(2,1)} %gather.7, f32[32,6]{1,0:T(8,128)S(1)} %copy.50, pred[32,6]{1,0:T(8,128)(4,1)S(1)} %get-tuple-element.5), kind=kLoop, calls=%fused_computation.8 | loop fusion | flops 1507328 | bytes 1049536 | tf_op jit(solution)/shard_map/reduce_sum | solution.py:72
  197.4 0.7 fusion.29
  (76 shorter events, 4.4 us)
Async XLA Ops:
  6.5 2.0 copy-start
  6.5 6.8 %copy-start.1 = (bf16[32,2048]{1,0:T(8,128)(2,1)S(1)}, bf16[32,2048]{1,0:T(8,128)(2,1)}, u32[]{:S(2)}) copy-start(bf16[32,2048]{1,0:T(8,128)(2,1)} %param.17) | copy-start | bytes 393220
  6.5 6.8 %copy-start.7 = (f32[2048]{0:T(1024)S(1)}, f32[2048]{0:T(1024)}, u32[]{:S(2)}) copy-start(f32[2048]{0:T(1024)} %param.19) | copy-start | bytes 24580
  6.5 6.6 %copy-start.12 = (s32[32]{0:T(128)S(1)}, s32[32]{0:T(128)}, u32[]{:S(2)}) copy-start(s32[32]{0:T(128)} %param.18) | copy-start | bytes 388
  6.5 6.8 %copy-start.6 = (bf16[64,2048]{1,0:T(8,128)(2,1)S(1)}, bf16[64,2048]{1,0:T(8,128)(2,1)}, u32[]{:S(2)}) copy-start(bf16[64,2048]{1,0:T(8,128)(2,1)} %param.23) | copy-start | bytes 786436
  6.5 46.8 %all-gather.3.cloned.1.call-start = ((), (), s32[]{:S(2)}) async-start(), calls=%async_computation.3 | async-start | bytes 1310720 | tf_op jit(solution)/shard_map/all_gather | solution.py:169
  12.3 4.2 %copy-start.3 = (bf16[2048,512]{1,0:T(8,128)(2,1)S(1)}, bf16[2048,512]{1,0:T(8,128)(2,1)}, u32[]{:S(2)}) copy-start(bf16[2048,512]{1,0:T(8,128)(2,1)} %param.21) | copy-start | bytes 6291460
  12.3 5.2 %copy-start.11 = (f32[512]{0:T(512)S(1)}, f32[512]{0:T(512)}, u32[]{:S(2)}) copy-start(f32[512]{0:T(512)} %param.22) | copy-start | bytes 6148
  13.2 3.9 %copy-start.4 = (bf16[4,512,128]{2,1,0:T(8,128)(2,1)S(1)}, bf16[4,512,128]{2,1,0:T(8,128)(2,1)}, u32[]{:S(2)}) copy-start(bf16[4,512,128]{2,1,0:T(8,128)(2,1)} %param.24) | copy-start | bytes 1572868
  13.2 3.9 %slice-start.2 = ((bf16[32,4,192]{2,1,0:T(4,128)(2,1)}), bf16[32,4,128]{2,1,0:T(4,128)(2,1)S(1)}, s32[]{:S(2)}) async-start(bf16[32,4,192]{2,1,0:T(4,128)(2,1)} %reshape.195), calls=%async_computation.6 | async-start | bytes 65536 | tf_op jit(solution)/shard_map/slice | solution.py:145
  13.3 10.6 %slice-start = ((s8[8388608]{0:T(1024)(128)(4,1)}), s8[4194304]{0:T(1024)(128)(4,1)S(1)}, s32[]{:S(2)}) async-start(s8[8388608]{0:T(1024)(128)(4,1)} %bitcast.66), calls=%async_computation.4 | async-start | bytes 8388608
  17.8 6.2 %slice-start.1 = ((s8[8388608]{0:T(1024)(128)(4,1)}), s8[4194304]{0:T(1024)(128)(4,1)S(1)}, s32[]{:S(2)}) async-start(s8[8388608]{0:T(1024)(128)(4,1)} %bitcast.66), calls=%async_computation.5 | async-start | bytes 8388608
  23.9 1.3 copy-start.5
  24.0 1.8 copy-start.2
  25.2 1.8 copy-start.9
  25.7 30.8 %copy-start.8 = (f32[2048]{0:T(1024)S(1)}, f32[2048]{0:T(1024)}, u32[]{:S(2)}) copy-start(f32[2048]{0:T(1024)} %param.29) | copy-start | bytes 24580
  26.9 160.7 %all-reduce.2.cloned.1.call-start = ((), (), s32[]{:S(2)}) async-start(), calls=%async_computation.2 | async-start | bytes 4194304 | tf_op jit(solution)/shard_map/psum | solution.py:181
  93.8 4.8 %copy-start.13 = (bf16[2,352,2048]{2,1,0:T(8,128)(2,1)S(1)}, bf16[2,352,2048]{2,1,0:T(8,128)(2,1)}, u32[]{:S(2)}) copy-start(bf16[2,352,2048]{2,1,0:T(8,128)(2,1)} %param.33) | copy-start | bytes 8650756
  132.2 0.7 copy-start.10
Sparse Core Ops, SparseCore 0:
  27.1 26.2 all-gather.2
  132.3 55.2 all-reduce.1
